TPU v7x, 256 devices: a whole 4x4x8 slice. The times are simulated.
256 devices in a mesh: row: 8 (over z), col: 32 (over y, x, core).
Axes of the slice: x: 4, y: 4, z: 8, core: 2. Of those that a mesh axis runs over, the one named last changes fastest.
Arguments:
- ancestor_inverse: bfloat16 [24576, 24576], P('row', 'col'), may hold values from -6 to 6
- factor_slots: bfloat16 [3, 16384, 512], P(None, ('row', 'col')), may hold values from -0.25 to 0.25
- slot_tiles: int32 [3, 64], replicated, may hold values from -1 to 95, as said below
- parent_factor: bfloat16 [2, 512, 512], replicated, may hold values from -0.25 to 0.25
- diag_inverse: float32 [3, 512, 512], replicated, may hold values from -6 to 6
Outputs:
- inverse_panels: bfloat16 [3, 24576, 512], P(None, ('row', 'col'))
- diag_blocks: float32 [3, 512, 512], replicated
- parent_blocks: float32 [2, 512, 512], replicated
Inputs may be any that keep to these rules, and one draw needn't show every extreme that they name: `slot_tiles`: entries b * 2 to b * 2 + 1 of a supernode's row are the slots of column block b: each is -1 (empty) or names a tile from b * 3 to b * 3 + 2, no tile twice; in each supernode some block has all its slots filled. `factor_slots`: rows of an empty slot are not part of the factor.
All inputs are finite; a program needn't handle non-finite values.
Results may differ from a plain program's by a relative error of at most 0.00075.
Values may be sent and summed in bfloat16 or wider, within the bound.
No kernel may reach another device: no remote copies, remote signals or barrier semaphores. Data moves between devices by JAX's collectives and lax.ppermute only.
A program may use at most 128 MiB of HBM per device.

v0:
```python
import jax
import jax.numpy as jnp
from jax import lax
from jax.sharding import PartitionSpec as P

TILE = 256
CAP = 2
exact_mode = lax.Precision.HIGHEST


def spread(shard, axis, root):
    mine = lax.axis_index(axis) == root
    return lax.psum(jnp.where(mine, shard, jnp.zeros_like(shard)), axis)


def padded_block(slot_data, slot_ids, block_index, tiles_per_block, tile_rows):
    local_tile = slot_ids - block_index * tiles_per_block
    pieces = []
    for tile_index in range(tiles_per_block):
        chosen = jnp.zeros((tile_rows, slot_data.shape[1]), slot_data.dtype)
        for member in range(slot_ids.shape[0]):
            chosen = jnp.where(
                local_tile[member] == tile_index,
                slot_data[member * tile_rows : (member + 1) * tile_rows],
                chosen,
            )
        pieces.append(chosen)
    return jnp.concatenate(pieces, axis=0)


def chosen_columns(inverse_block, slot_ids, block_index, tiles_per_block, tile_rows):
    local_tile = jnp.clip(slot_ids - block_index * tiles_per_block, 0, tiles_per_block - 1)
    pieces = [
        lax.dynamic_slice_in_dim(inverse_block, local_tile[member] * tile_rows, tile_rows, 1)
        for member in range(slot_ids.shape[0])
    ]
    return jnp.concatenate(pieces, axis=1)


def masked_rows(slot_data, slot_ids, tile_rows):
    live_rows = jnp.repeat(slot_ids >= 0, tile_rows)
    return jnp.where(live_rows[:, None], slot_data, jnp.zeros_like(slot_data))


def on_device(ancestor_inverse, factor_slots, slot_tiles, parent_factor, diag_inverse):
    row_count = lax.axis_size("row")
    col_count = lax.axis_size("col")
    row_index = lax.axis_index("row")
    col_index = lax.axis_index("col")
    block_rows, block_cols = ancestor_inverse.shape
    tile_rows = TILE
    tiles_per_block = block_cols // tile_rows
    node_count = factor_slots.shape[0]
    slot_count = CAP
    slot_rows = slot_count * tile_rows
    groups_per_row = col_count // row_count
    panel_rows = block_rows // col_count
    own_block = row_index * groups_per_row + col_index // row_count
    own_offset = col_index % row_count * panel_rows
    slot_start = col_index % groups_per_row * slot_rows
    owner_row = col_index // groups_per_row

    def finish(node, first_total, second_total, prev_diag):
        if node == 0:
            return (diag_inverse[0] - first_total, None)
        parent_link = parent_factor[node - 1].astype(jnp.float32)
        upper = -(second_total + jnp.dot(prev_diag, parent_link, precision=exact_mode))
        diagonal = (
            diag_inverse[node] - first_total - jnp.dot(parent_link.T, upper, precision=exact_mode)
        )
        return (diagonal, upper)

    def node_sums(node, first_part, second_part):
        if node == 0:
            return (lax.psum(first_part, ("row", "col")), None)
        return lax.psum((first_part, second_part), ("row", "col"))

    panels = []
    diagonals = []
    parents = []
    previous = None
    prev_diag = None
    for node in range(node_count):
        row_slots = lax.all_gather(factor_slots[node], "col", axis=0, tiled=True)
        mine = lax.dynamic_slice_in_dim(row_slots, slot_start, slot_rows, 0)
        col_slots = spread(mine, "row", owner_row)
        tiles_node = slot_tiles[node]
        col_ids = lax.dynamic_slice_in_dim(tiles_node, col_index * slot_count, slot_count)
        prepare_columns = chosen_columns(
            ancestor_inverse, col_ids, col_index, tiles_per_block, tile_rows
        )
        prepare_weights = masked_rows(col_slots, col_ids, tile_rows)
        own_ids = lax.dynamic_slice_in_dim(tiles_node, own_block * slot_count, slot_count)
        own_slots = lax.dynamic_slice_in_dim(
            row_slots, col_index // row_count * slot_rows, slot_rows, 0
        )
        own_padded = padded_block(own_slots, own_ids, own_block, tiles_per_block, tile_rows)
        own_rows = lax.dynamic_slice_in_dim(own_padded, own_offset, panel_rows, 0)
        row_padded = None
        columns, weights, own_rows, row_padded = (
            prepare_columns,
            prepare_weights,
            own_rows.astype(jnp.float32),
            row_padded,
        )
        second_part = None
        if node > 0:
            second_part = jnp.dot(previous.T, own_rows, precision=exact_mode)
        summed = lax.psum_scatter(
            jnp.dot(columns, weights, preferred_element_type=jnp.float32),
            "col",
            scatter_dimension=0,
            tiled=True,
        )
        column = -summed
        if node > 0:
            advance_parent_link = parent_factor[node - 1].astype(jnp.float32)
            column = column - jnp.dot(previous, advance_parent_link, precision=exact_mode)
        first_part = jnp.dot(own_rows.T, column, precision=exact_mode)
        first_total, second_total = node_sums(node, first_part, second_part)
        diagonal, upper = finish(node, first_total, second_total, prev_diag)
        panels.append(column.astype(jnp.bfloat16))
        diagonals.append(diagonal)
        if node > 0:
            parents.append(upper)
        previous = column
        prev_diag = diagonal
    return (jnp.stack(panels), jnp.stack(diagonals), jnp.stack(parents))


def solution(mesh):
    placed = (P("row", "col"), P(None, ("row", "col"), None), P(), P(), P())
    return jax.shard_map(
        on_device,
        mesh=mesh,
        in_specs=placed,
        out_specs=(P(None, ("row", "col"), None), P(), P()),
        check_vma=False,
    )
```

profile of v0, /device:TPU:8, one launch (start us, length us, event | category | flops | bytes accessed | tf_op | source)
XLA Modules:
  0.0 841.9 jit_solution(13287973406344088835)
XLA Ops:
  7.2 0.0 all-gather.9.cloned.1.call-start
  7.2 1.6 fusion.71
  8.8 0.0 all-gather.9.cloned.1.call-update
  8.8 0.0 all-gather.7.cloned.1.call-start
  8.9 0.7 all-gather.7.cloned.1.call-update
  9.6 0.0 all-gather.11.cloned.1.call-start
  9.6 0.7 all-gather.11.cloned.1.call-update
  10.3 0.0 all-reduce.7.cloned.1.call-start
  10.4 51.9 %all-gather.9.cloned.1.call-done = bf16[1,2048,512]{2,1,0:T(8,128)(2,1)} async-done(((bf16[1,64,512]{2,1,0:T(8,128)(2,1)}), bf16[1,2048,512]{2,1,0:T(8,128)(2,1)}) %all-gather.9.cloned.1.call-update) | async-done | bytes 2097168 | tf_op jit(solution)/shard_map/all_gather | solution.py:84
  62.3 1.9 select_bitcast_fusion.1
  64.2 49.2 %all-gather.7.cloned.1.call-done = bf16[1,2048,512]{2,1,0:T(8,128)(2,1)} async-done(((bf16[1,64,512]{2,1,0:T(8,128)(2,1)}), bf16[1,2048,512]{2,1,0:T(8,128)(2,1)}) %all-gather.7.cloned.1.call-update) | async-done | bytes 2097168 | tf_op jit(solution)/shard_map/all_gather | solution.py:84
  113.4 1.9 select_bitcast_fusion.2
  115.3 49.2 %all-gather.11.cloned.1.call-done = bf16[1,2048,512]{2,1,0:T(8,128)(2,1)} async-done(((bf16[1,64,512]{2,1,0:T(8,128)(2,1)}), bf16[1,2048,512]{2,1,0:T(8,128)(2,1)}) %all-gather.11.cloned.1.call-update) | async-done | bytes 2097168 | tf_op jit(solution)/shard_map/all_gather | solution.py:84
  164.5 1.9 select_bitcast_fusion
  166.4 0.0 all-reduce.7.cloned.1.call-update
  166.5 0.0 reduce-scatter.6.cloned.1.call-start
  166.6 0.1 fusion.56
  166.6 0.6 fusion.75
  168.5 0.1 fusion.54
  168.6 0.6 fusion.77
  170.4 0.7 fusion.78
  172.4 0.1 compare_bitcast_fusion
  172.5 0.1 broadcast_in_dim.36
  172.6 6.8 constant_dynamic-slice_fusion.4
  179.5 66.0 %all-reduce.7.cloned.1.call-done = (bf16[512,512]{1,0:T(8,128)(2,1)}, bf16[512,512]{1,0:T(8,128)(2,1)}, bf16[512,512]{1,0:T(8,128)(2,1)}) async-done(((bf16[512,512]{1,0:T(8,128)(2,1)}, bf16[512,512]{1,0:T(8,128)(2,1)}, bf16[512,512]{1,0:T(8,128)(2,1)}), (bf16[512,512]{1,0:T(8,128)(2,1)}, bf16[512,512]{1,0:T(8,128)(2,1)}, bf16[512,512]{1,0:T(8,128)(2,1)})) %all-reduce.7.cloned.1.call-update) | async-done | bytes 1572880 | tf_op jit(solution)/shard_map/psum | solution.py:13
  245.4 6.5 fusion.4
  251.9 0.0 reduce-scatter.6.cloned.1.call-update
  252.0 0.0 reduce-scatter.4.cloned.1.call-start
  252.0 0.1 compare_bitcast_fusion.2
  252.1 0.1 broadcast_in_dim.33
  252.2 6.5 fusion
  258.7 0.0 reduce-scatter.4.cloned.1.call-update
  258.7 0.0 reduce-scatter.8.cloned.1.call-start
  258.7 0.1 broadcast_in_dim.39
  258.8 5.5 fusion.8
  264.3 0.0 reduce-scatter.8.cloned.1.call-update
  264.4 0.2 all-reduce.5.cloned.1.call-start
  264.6 0.6 fusion.73
  272.8 0.6 fusion.74
  277.3 1.2 select_bitcast_fusion.8
  278.5 2.0 select_bitcast_fusion.10
  280.5 1.2 select_bitcast_fusion.5
  281.7 63.3 %reduce-scatter.6.cloned.1.call-done = f32[96,512]{1,0:T(8,128)} async-done(((f32[3072,512]{1,0:T(8,128)}), f32[96,512]{1,0:T(8,128)}) %reduce-scatter.6.cloned.1.call-update) | async-done | bytes 196624 | tf_op jit(solution)/shard_map/reduce_scatter | solution.py:109
  345.0 97.1 %reduce-scatter.4.cloned.1.call-done = f32[96,512]{1,0:T(8,128)} async-done(((f32[3072,512]{1,0:T(8,128)}), f32[96,512]{1,0:T(8,128)}) %reduce-scatter.4.cloned.1.call-update) | async-done | bytes 196624 | tf_op jit(solution)/shard_map/reduce_scatter | solution.py:109
  442.1 1.4 convolution_subtract_fusion.1
  443.5 1.7 fusion.69
  445.2 94.2 %reduce-scatter.8.cloned.1.call-done = f32[96,512]{1,0:T(8,128)} async-done(((f32[3072,512]{1,0:T(8,128)}), f32[96,512]{1,0:T(8,128)}) %reduce-scatter.8.cloned.1.call-update) | async-done | bytes 196624 | tf_op jit(solution)/shard_map/reduce_scatter | solution.py:109
  539.4 1.3 convolution_subtract_fusion
  540.7 1.7 fusion.67
  542.5 1.7 fusion.64
  544.2 1.7 fusion.39
  545.8 1.8 fusion.41
  547.7 0.0 all-reduce.5.cloned.1.call-update
  547.8 0.7 pad_maximum_fusion.2
  548.5 274.5 %all-reduce.5.cloned.1.call-done = (f32[512,512]{1,0:T(8,128)}, f32[512,512]{1,0:T(8,128)}, f32[512,512]{1,0:T(8,128)}, f32[512,512]{1,0:T(8,128)}, f32[512,512]{1,0:T(8,128)}) async-done(((f32[512,512]{1,0:T(8,128)}, f32[512,512]{1,0:T(8,128)}, f32[512,512]{1,0:T(8,128)}, f32[512,512]{1,0:T(8,128)}, f32[512,512]{1,0:T(8,128)}), (f32[512,512]{1,0:T(8,128)}, f32[512,512]{1,0:T(8,128)}, f32[512,512]{1,0:T(8,128)}, ...) | async-done | bytes 5242896 | tf_op jit(solution)/shard_map/psum | solution.py:76
  823.1 1.9 fusion.29
  825.0 0.6 copy-done.1
  825.6 2.6 fusion.13
  828.2 1.1 fusion.16
  829.3 0.1 copy-done.3
  829.4 1.0 fusion.12
  830.4 1.1 fusion.15
  831.5 1.5 pad_maximum_fusion.1
  833.0 2.0 pad_maximum_fusion
  (23 shorter events, 0.2 us)
Async XLA Ops:
  7.2 159.4 %copy-start.8 = (s32[3,64]{1,0:T(4,128)S(1)}, s32[3,64]{1,0:T(4,128)}, u32[]{:S(2)}) copy-start(s32[3,64]{1,0:T(4,128)} %param.7) | copy-start | bytes 2308
  7.2 55.1 %all-gather.9.cloned.1.call-start = ((), (), s32[]{:S(2)}) async-start(), calls=%async_computation.7 | async-start | bytes 2162688 | tf_op jit(solution)/shard_map/all_gather | solution.py:84
  8.8 104.6 %all-gather.7.cloned.1.call-start = ((), (), s32[]{:S(2)}) async-start(), calls=%async_computation.6 | async-start | bytes 2162688 | tf_op jit(solution)/shard_map/all_gather | solution.py:84
  9.6 154.9 %all-gather.11.cloned.1.call-start = ((), (), s32[]{:S(2)}) async-start(), calls=%async_computation.8 | async-start | bytes 2162688 | tf_op jit(solution)/shard_map/all_gather | solution.py:84
  10.3 235.1 %all-reduce.7.cloned.1.call-start = ((), (), s32[]{:S(2)}) async-start(), calls=%async_computation.10 | async-start | bytes 3145728 | tf_op jit(solution)/shard_map/psum | solution.py:13
  166.5 178.5 %reduce-scatter.6.cloned.1.call-start = ((), (), s32[]{:S(2)}) async-start(), calls=%async_computation.4 | async-start | bytes 6488064 | tf_op jit(solution)/shard_map/reduce_scatter | solution.py:109
  252.0 190.1 %reduce-scatter.4.cloned.1.call-start = ((), (), s32[]{:S(2)}) async-start(), calls=%async_computation.3 | async-start | bytes 6488064 | tf_op jit(solution)/shard_map/reduce_scatter | solution.py:109
  258.7 280.7 %reduce-scatter.8.cloned.1.call-start = ((), (), s32[]{:S(2)}) async-start(), calls=%async_computation.5 | async-start | bytes 6488064 | tf_op jit(solution)/shard_map/reduce_scatter | solution.py:109
  264.4 177.7 %copy-start = (bf16[2,512,512]{2,1,0:T(8,128)(2,1)S(1)}, bf16[2,512,512]{2,1,0:T(8,128)(2,1)}, u32[]{:S(2)}) copy-start(bf16[2,512,512]{2,1,0:T(8,128)(2,1)} %param.8) | copy-start | bytes 3145732
  264.4 558.7 %all-reduce.5.cloned.1.call-start = ((), (), s32[]{:S(2)}) async-start(), calls=%async_computation.9 | async-start | bytes 10485760 | tf_op jit(solution)/shard_map/psum | solution.py:76
  443.5 100.7 %copy-start.2 = (f32[96,512]{1,0:T(8,128)S(1)}, f32[96,512]{1,0:T(8,128)}, u32[]{:S(2)}) copy-start(f32[96,512]{1,0:T(8,128)} %reduce-scatter.4.cloned.1.call-done) | copy-start | bytes 589828
  540.7 5.1 copy-start.4
  540.7 5.1 copy-start.5
  823.0 2.5 copy-start.1
  825.0 3.2 copy-start.7
  828.2 1.2 copy-start.3
  828.2 2.2 copy-start.6
Sparse Core Ops, SparseCore 0:
  11.1 51.0 all-gather.8
  65.4 47.9 all-gather.6
  116.5 47.9 all-gather.10
  167.0 78.4 all-reduce.6
  252.1 92.8 reduce-scatter.5
  348.9 93.1 reduce-scatter.3
  446.1 93.2 reduce-scatter.7
  547.8 275.1 all-reduce.4
where the time goes:
time: 843 us; the launch traced here: 842 us
  waiting for transfers between devices  747 us (89%)
  matrix products  35.6 us (4%)
  between operations  29.7 us (4%)
  other arithmetic  16.8 us (2%)
  local copies, waits for them, and re-layouts  12.5 us (1%)
    psum x1, waiting for transfers between devices, node_sums(): return lax.psum((first_part, second_part), ('row', 'col'))  275 us
    reduce_scatter x3, waiting for transfers between devices, on_device(): lax.psum_scatter(jnp.dot(columns, weights, preferred_element_type=jnp.flo...  255 us
    all_gather x3, waiting for transfers between devices, on_device(): row_slots = lax.all_gather(factor_slots[node], 'col', axis=0, tiled=True)  150 us
    psum x1, waiting for transfers between devices, spread(): return lax.psum(jnp.where(mine, shard, jnp.zeros_like(shard)), axis)  66 us
    dot_general x3, matrix products, on_device(): jnp.dot(columns, weights, preferred_element_type=jnp.float32)  18.5 us
  transfers between devices with their start and end apart: 8, of which 8 were waited for; matrix products, arithmetic and copies ran while one was open for 4% of the time, Pallas kernels for 0%

commit v1 on v0

--- a/solution.py
+++ b/solution.py
@@ -81,7 +81,9 @@
     previous = None
     prev_diag = None
     for node in range(node_count):
-        row_slots = lax.all_gather(factor_slots[node], "col", axis=0, tiled=True)
+        x = factor_slots[node]
+        repeated = jnp.stack([x] * lax.axis_size("col"))
+        row_slots = jnp.concatenate(lax.all_to_all(repeated, "col", 0, 0), axis=0)
         mine = lax.dynamic_slice_in_dim(row_slots, slot_start, slot_rows, 0)
         col_slots = spread(mine, "row", owner_row)
         tiles_node = slot_tiles[node]

time: 843 us -> 788 us (0.935)
  waiting for transfers between devices: 747 us -> 616 us
  blocking collectives: 0 us -> 65.5 us
    all_gather x3 -> x0, waiting for transfers between devices: 150 us -> none  [on_device(): row_slots = lax.all_gather(factor_slots[node], 'col', axis=0, tiled=True)]
    all_to_all x0 -> x2, blocking collectives: none -> 65.5 us  [on_device(): row_slots = jnp.concatenate(lax.all_to_all(repeated, 'col', 0, 0), axis=0)]
    all_to_all x0 -> x1, waiting for transfers between devices: none -> 22.7 us  [on_device(): row_slots = jnp.concatenate(lax.all_to_all(repeated, 'col', 0, 0), axis=0)]
  transfers between devices with their start and end apart: 8 -> 6, of which waited for: 8 -> 6; matrix products, arithmetic and copies ran while one was open for 4% -> 5% of each run, Pallas kernels for 0% -> 0%
where the time goes in v1:
time: 788 us; the launch traced here: 787 us
  waiting for transfers between devices  616 us (78%)
  blocking collectives  65.5 us (8%)
  matrix products  36.2 us (5%)
  between operations  29.7 us (4%)
  local copies, waits for them, and re-layouts  16.3 us (2%)
  other arithmetic  16.3 us (2%)
    psum x1, waiting for transfers between devices, node_sums(): return lax.psum((first_part, second_part), ('row', 'col'))  275 us
    reduce_scatter x3, waiting for transfers between devices, on_device(): lax.psum_scatter(jnp.dot(columns, weights, preferred_element_type=jnp.flo...  251 us
    psum x1, waiting for transfers between devices, spread(): return lax.psum(jnp.where(mine, shard, jnp.zeros_like(shard)), axis)  66.9 us
    all_to_all x2, blocking collectives, on_device(): row_slots = jnp.concatenate(lax.all_to_all(repeated, 'col', 0, 0), axis=0)  65.5 us
    all_to_all x1, waiting for transfers between devices, on_device(): row_slots = jnp.concatenate(lax.all_to_all(repeated, 'col', 0, 0), axis=0)  22.7 us
    dot_general x3, matrix products, on_device(): jnp.dot(columns, weights, preferred_element_type=jnp.float32)  19.2 us
  transfers between devices with their start and end apart: 6, of which 6 were waited for; matrix products, arithmetic and copies ran while one was open for 5% of the time, Pallas kernels for 0%

profile of v1, /device:TPU:8, one launch (start us, length us, event | category | flops | bytes accessed | tf_op | source)
XLA Modules:
  0.0 787.3 jit_solution(2439904288077776930)
XLA Ops:
  7.2 0.9 slice_bitcast_fusion
  8.1 0.2 stack.46
  8.3 33.5 %all_to_all.15 = bf16[32,64,512]{2,1,0:T(8,128)(2,1)} all-to-all(bf16[32,64,512]{2,1,0:T(8,128)(2,1)S(1)} %stack.46), channel_id=1, replica_groups=mesh['row'=8,'col'=32] {'col'}, dimensions={0} | all-to-all | bytes 4194304 | tf_op jit(solution)/shard_map/all_to_all | solution.py:86
  41.8 0.2 stack.42
  42.1 32.0 %all_to_all.16 = bf16[32,64,512]{2,1,0:T(8,128)(2,1)} all-to-all(bf16[32,64,512]{2,1,0:T(8,128)(2,1)S(1)} %stack.42), channel_id=1, replica_groups=mesh['row'=8,'col'=32] {'col'}, dimensions={0} | all-to-all | bytes 4194304 | tf_op jit(solution)/shard_map/all_to_all | solution.py:86
  74.1 1.6 stack.44
  75.6 6.5 all-to-all-start.1
  82.1 0.0 all-reduce.7.cloned.1.call-start
  82.2 1.9 dynamic-slice_select_fusion
  84.1 1.9 dynamic-slice_select_fusion.2
  86.0 22.7 %all-to-all-done.1 = bf16[32,64,512]{2,1,0:T(8,128)(2,1)S(1)} async-done(((bf16[32,64,512]{2,1,0:T(8,128)(2,1)}), bf16[32,64,512]{2,1,0:T(8,128)(2,1)S(1)}, u32[]{:S(2)}, u32[]{:S(2)}) %all-to-all-start.1) | async-done | bytes 2097184 | tf_op jit(solution)/shard_map/all_to_all | solution.py:86
  108.7 0.9 dynamic-slice_select_fusion.1
  109.6 0.0 all-reduce.7.cloned.1.call-update
  109.6 0.0 reduce-scatter.6.cloned.1.call-start
  109.7 0.1 fusion.56
  109.8 0.6 fusion.74
  111.7 0.1 fusion.54
  111.7 0.6 fusion.76
  113.7 0.6 fusion.77
  115.6 0.1 compare_bitcast_fusion
  115.7 0.1 broadcast_in_dim.36
  115.7 7.7 constant_dynamic-slice_fusion.4
  123.5 66.9 %all-reduce.7.cloned.1.call-done = (bf16[512,512]{1,0:T(8,128)(2,1)}, bf16[512,512]{1,0:T(8,128)(2,1)}, bf16[512,512]{1,0:T(8,128)(2,1)}) async-done(((bf16[512,512]{1,0:T(8,128)(2,1)}, bf16[512,512]{1,0:T(8,128)(2,1)}, bf16[512,512]{1,0:T(8,128)(2,1)}), (bf16[512,512]{1,0:T(8,128)(2,1)}, bf16[512,512]{1,0:T(8,128)(2,1)}, bf16[512,512]{1,0:T(8,128)(2,1)})) %all-reduce.7.cloned.1.call-update) | async-done | bytes 1572880 | tf_op jit(solution)/shard_map/psum | solution.py:13
  190.4 6.5 fusion.4
  196.9 0.0 reduce-scatter.6.cloned.1.call-update
  196.9 0.0 reduce-scatter.4.cloned.1.call-start
  197.0 0.1 compare_bitcast_fusion.2
  197.0 0.1 broadcast_in_dim.33
  197.1 0.8 copy-done.14
  197.9 6.4 fusion
  204.3 0.0 reduce-scatter.4.cloned.1.call-update
  204.3 0.0 reduce-scatter.8.cloned.1.call-start
  204.4 0.1 broadcast_in_dim.39
  204.5 0.9 copy-done.13
  205.3 6.3 fusion.8
  211.7 0.0 reduce-scatter.8.cloned.1.call-update
  211.7 0.2 all-reduce.5.cloned.1.call-start
  212.0 0.6 fusion.72
  220.3 0.6 fusion.73
  224.8 2.0 select_select_fusion.2
  226.9 2.1 select_select_fusion.7
  228.9 1.0 select_select_fusion.5
  229.9 60.0 %reduce-scatter.6.cloned.1.call-done = f32[96,512]{1,0:T(8,128)} async-done(((f32[3072,512]{1,0:T(8,128)}), f32[96,512]{1,0:T(8,128)}) %reduce-scatter.6.cloned.1.call-update) | async-done | bytes 196624 | tf_op jit(solution)/shard_map/reduce_scatter | solution.py:111
  290.0 97.3 %reduce-scatter.4.cloned.1.call-done = f32[96,512]{1,0:T(8,128)} async-done(((f32[3072,512]{1,0:T(8,128)}), f32[96,512]{1,0:T(8,128)}) %reduce-scatter.4.cloned.1.call-update) | async-done | bytes 196624 | tf_op jit(solution)/shard_map/reduce_scatter | solution.py:111
  387.3 1.4 convolution_subtract_fusion.1
  388.7 1.6 fusion.69
  390.3 94.1 %reduce-scatter.8.cloned.1.call-done = f32[96,512]{1,0:T(8,128)} async-done(((f32[3072,512]{1,0:T(8,128)}), f32[96,512]{1,0:T(8,128)}) %reduce-scatter.8.cloned.1.call-update) | async-done | bytes 196624 | tf_op jit(solution)/shard_map/reduce_scatter | solution.py:111
  484.4 1.3 convolution_subtract_fusion
  485.7 1.7 fusion.67
  487.4 1.7 fusion.64
  489.2 1.7 fusion.39
  490.8 1.8 fusion.41
  492.7 0.0 all-reduce.5.cloned.1.call-update
  492.8 0.7 pad_maximum_fusion.2
  493.5 275.3 %all-reduce.5.cloned.1.call-done = (f32[512,512]{1,0:T(8,128)}, f32[512,512]{1,0:T(8,128)}, f32[512,512]{1,0:T(8,128)}, f32[512,512]{1,0:T(8,128)}, f32[512,512]{1,0:T(8,128)}) async-done(((f32[512,512]{1,0:T(8,128)}, f32[512,512]{1,0:T(8,128)}, f32[512,512]{1,0:T(8,128)}, f32[512,512]{1,0:T(8,128)}, f32[512,512]{1,0:T(8,128)}), (f32[512,512]{1,0:T(8,128)}, f32[512,512]{1,0:T(8,128)}, f32[512,512]{1,0:T(8,128)}, ...) | async-done | bytes 5242896 | tf_op jit(solution)/shard_map/psum | solution.py:76
  768.8 1.9 fusion.29
  770.8 0.6 copy-done.1
  771.4 2.6 fusion.13
  774.0 1.1 fusion.16
  775.1 0.1 copy-done.6
  775.2 1.0 fusion.12
  776.2 1.1 fusion.15
  777.3 1.5 pad_maximum_fusion.1
  778.8 2.0 pad_maximum_fusion
  (33 shorter events, 0.2 us)
Async XLA Ops:
  75.6 33.1 %all-to-all-start.1 = ((bf16[32,64,512]{2,1,0:T(8,128)(2,1)}), bf16[32,64,512]{2,1,0:T(8,128)(2,1)S(1)}, u32[]{:S(2)}, u32[]{:S(2)}) async-start(bf16[32,64,512]{2,1,0:T(8,128)(2,1)} %stack.44), calls=%async_computation.2 | async-start | bytes 4194304 | tf_op jit(solution)/shard_map/all_to_all | solution.py:86
  82.1 27.6 %copy-start.12 = (s32[3,64]{1,0:T(4,128)S(1)}, s32[3,64]{1,0:T(4,128)}, u32[]{:S(2)}) copy-start(s32[3,64]{1,0:T(4,128)} %param.7) | copy-start | bytes 2308
  82.1 108.3 %all-reduce.7.cloned.1.call-start = ((), (), s32[]{:S(2)}) async-start(), calls=%async_computation.10 | async-start | bytes 3145728 | tf_op jit(solution)/shard_map/psum | solution.py:13
  109.6 180.4 %reduce-scatter.6.cloned.1.call-start = ((), (), s32[]{:S(2)}) async-start(), calls=%async_computation.7 | async-start | bytes 6488064 | tf_op jit(solution)/shard_map/reduce_scatter | solution.py:111
  196.9 1.0 copy-start.14
  196.9 190.4 %reduce-scatter.4.cloned.1.call-start = ((), (), s32[]{:S(2)}) async-start(), calls=%async_computation.6 | async-start | bytes 6488064 | tf_op jit(solution)/shard_map/reduce_scatter | solution.py:111
  204.3 1.0 copy-start.13
  204.3 280.1 %reduce-scatter.8.cloned.1.call-start = ((), (), s32[]{:S(2)}) async-start(), calls=%async_computation.8 | async-start | bytes 6488064 | tf_op jit(solution)/shard_map/reduce_scatter | solution.py:111
  211.7 175.5 %copy-start = (bf16[2,512,512]{2,1,0:T(8,128)(2,1)S(1)}, bf16[2,512,512]{2,1,0:T(8,128)(2,1)}, u32[]{:S(2)}) copy-start(bf16[2,512,512]{2,1,0:T(8,128)(2,1)} %param.8) | copy-start | bytes 3145732
  211.7 557.1 %all-reduce.5.cloned.1.call-start = ((), (), s32[]{:S(2)}) async-start(), calls=%async_computation.9 | async-start | bytes 10485760 | tf_op jit(solution)/shard_map/psum | solution.py:76
  229.9 257.5 %copy-start.3 = (bf16[256,512]{1,0:T(8,128)(2,1)S(1)}, bf16[256,512]{1,0:T(8,128)(2,1)}, u32[]{:S(2)}) copy-start(bf16[256,512]{1,0:T(8,128)(2,1)} %get-tuple-element.20) | copy-start | bytes 786436
  229.9 257.5 %copy-start.4 = (bf16[256,512]{1,0:T(8,128)(2,1)S(1)}, bf16[256,512]{1,0:T(8,128)(2,1)}, u32[]{:S(2)}) copy-start(bf16[256,512]{1,0:T(8,128)(2,1)} %get-tuple-element.21) | copy-start | bytes 786436
  229.9 257.5 %copy-start.5 = (bf16[256,512]{1,0:T(8,128)(2,1)S(1)}, bf16[256,512]{1,0:T(8,128)(2,1)}, u32[]{:S(2)}) copy-start(bf16[256,512]{1,0:T(8,128)(2,1)} %get-tuple-element.22) | copy-start | bytes 786436
  388.7 100.5 %copy-start.2 = (f32[96,512]{1,0:T(8,128)S(1)}, f32[96,512]{1,0:T(8,128)}, u32[]{:S(2)}) copy-start(f32[96,512]{1,0:T(8,128)} %reduce-scatter.4.cloned.1.call-done) | copy-start | bytes 589828
  485.7 5.1 copy-start.7
  485.7 5.1 copy-start.8
  485.7 5.1 copy-start.9
  768.8 2.5 copy-start.1
  770.7 3.2 copy-start.11
  773.9 1.2 copy-start.6
  774.0 2.2 copy-start.10
Sparse Core Ops, SparseCore 0:
  109.7 80.6 all-reduce.6
  197.0 92.8 reduce-scatter.5
  294.0 93.2 reduce-scatter.3
  391.1 93.2 reduce-scatter.7
  492.8 275.9 all-reduce.4
